TPU v7x, 128 devices: a whole 4x4x4 slice. The times are simulated.
128 devices in a mesh: tm: 32 (over x, z, core), tp: 4 (over y).
Axes of the slice: x: 4, y: 4, z: 4, core: 2. Of those that a mesh axis runs over, the one named last changes fastest.
Arguments:
- trajectory: float32 [64, 128, 3072], P('tm', None, 'tp'), may hold values from -6 to 6
- offset: int32 [1], replicated, may hold values from 0 to 63
- step_gaps: int32 [64], P('tm'), may hold values from 1 to 4, as said below
- qkv_weight: bfloat16 [3072, 3, 3072], P(None, None, 'tp')
- out_weight: bfloat16 [3072, 3072], P('tp'), may hold values from -4 to 4
- mod_weight: bfloat16 [256, 3, 3072], P(None, None, 'tp'), may hold values from -0.375 to 0.375
Outputs:
- advanced: float32 [64, 128, 3072], P('tm', None, 'tp')
Inputs may be any that keep to these rules, and one draw needn't show every extreme that they name: `step_gaps`: in aligned blocks of 2 timesteps, the gaps of block b sum to an even number for even b and to an odd number for odd b.
All inputs are finite; a program needn't handle non-finite values.
Results may differ from a plain program's by a relative error of at most 0.007.
Values may be sent and summed in bfloat16 or wider, within the bound.
No kernel may reach another device: no remote copies, remote signals or barrier semaphores. Data moves between devices by JAX's collectives and lax.ppermute only.
A program may use at most 128 MiB of HBM per device.

v0:
```python
import math
import jax
import jax.numpy as jnp
from jax import lax
from jax.sharding import PartitionSpec as P

HD = 128
FREQ = 256
ITERS = 2


def prefix(array, axis, combine, identity):
    size, place = (lax.axis_size(axis), lax.axis_index(axis))
    everything = lax.all_gather(array, axis)
    start = jnp.broadcast_to(jnp.asarray(identity, array.dtype), array.shape)

    def turn(k, before):
        reached = k < place
        new = combine(before, everything[k])
        return jnp.where(reached, new, before)

    return lax.fori_loop(0, size, turn, start)


def broadcast(block, axis, holder):
    block = jnp.where(lax.axis_index(axis) == holder, block, jnp.zeros_like(block))
    return lax.psum(block, axis)


def prefix_2(array, axis, join, neutral):
    place = lax.axis_index(axis)
    gathered = lax.all_gather(array.astype(jnp.bfloat16), axis)
    state = jnp.zeros_like(array) + jnp.asarray(neutral, array.dtype)

    def one(turn, state):
        return join(state, lax.dynamic_index_in_dim(gathered, turn, 0, False).astype(array.dtype))

    return lax.fori_loop(0, place, one, state)


def add_up(earlier, later):
    return earlier + later


def embedding(sigma):
    half_freq = FREQ // 2
    frequencies = jnp.exp(-math.log(10000.0) * jnp.arange(half_freq, dtype=jnp.float32) / half_freq)
    angles = 1000.0 * sigma[:, None] * frequencies[None, :]
    return jnp.concatenate([jnp.cos(angles), jnp.sin(angles)], -1).astype(jnp.bfloat16)


def body(trajectory, offset, step_gaps, qkv_weight, out_weight, mod_weight):
    steps_here, tok_count, col_count = trajectory.shape
    full_width = qkv_weight.shape[0]
    time_count = steps_here * lax.axis_size("tm")
    level_count = 5 * time_count
    before = prefix(jnp.sum(step_gaps), "tm", add_up, jnp.int32(0))
    levels = (offset[0] + before + jnp.cumsum(step_gaps) - step_gaps).astype(jnp.float32)
    sigma = 1.0 - levels / level_count
    step_size = step_gaps.astype(jnp.float32) / level_count
    embed_rows = embedding(sigma)
    full_mod = lax.all_gather(mod_weight, "tp", axis=2, tiled=True)
    modulation = jnp.dot(
        embed_rows, full_mod.reshape(FREQ, 3 * full_width), preferred_element_type=jnp.float32
    ).reshape(steps_here, 3, full_width)
    gate_rows = lax.dynamic_slice_in_dim(
        modulation[:, 2], lax.axis_index("tp") * col_count, col_count, 1
    )
    base_point = broadcast(trajectory[0], "tm", 0)
    flat_qkv = qkv_weight.reshape(full_width, -1)
    states = trajectory
    points = trajectory
    for sweep in range(ITERS):
        whole_rows = lax.all_gather(states, "tp", axis=2, tiled=True)
        row_mean = jnp.sum(whole_rows, -1, keepdims=True) / full_width
        variance = (
            jnp.sum(whole_rows * whole_rows, -1, keepdims=True) / full_width - row_mean * row_mean
        )
        inv_std = lax.rsqrt(variance + 1e-06)
        normed = (
            (whole_rows - row_mean) * inv_std * (1.0 + modulation[:, 1][:, None, :])
            + modulation[:, 0][:, None, :]
        ).astype(jnp.bfloat16)
        projected = jnp.einsum("std,de->ste", normed, flat_qkv, preferred_element_type=jnp.float32)
        projected = projected.astype(jnp.bfloat16).reshape(steps_here, tok_count, 3, -1, HD)
        queries = projected[:, :, 0]
        key_rows = projected[:, :, 1]
        values = projected[:, :, 2]
        scores = jnp.einsum(
            "sqhd,skhd->shqk", queries, key_rows, preferred_element_type=jnp.float32
        ) * (1.0 / math.sqrt(HD))
        row_max = jnp.max(scores, -1, keepdims=True)
        weights_exp = jnp.exp(scores - row_max)
        probs = (weights_exp / jnp.sum(weights_exp, -1, keepdims=True)).astype(jnp.bfloat16)
        attended = jnp.einsum(
            "shqk,skhd->sqhd", probs, values, preferred_element_type=jnp.float32
        ).astype(jnp.bfloat16)
        attended = attended.reshape(steps_here, tok_count, -1)
        head_out = jnp.einsum(
            "sqe,ed->sqd", attended, out_weight, preferred_element_type=jnp.float32
        )
        col_share = lax.psum_scatter(
            head_out.astype(jnp.bfloat16), "tp", scatter_dimension=2, tiled=True
        ).astype(jnp.float32)
        drifts = gate_rows[:, None, :] * col_share
        increments = -step_size[:, None, None] * drifts
        local_cum = jnp.cumsum(increments, 0)
        prefix_sum = prefix_2(
            local_cum[-1], "tm", add_up, jnp.zeros((tok_count, col_count), jnp.float32)
        )
        entry_point = prefix_sum + base_point
        points = entry_point[None] + local_cum
        states = jnp.concatenate([entry_point[None], points[:-1]], 0)
    return points


def solution(mesh):
    placed = (
        P("tm", None, "tp"),
        P(),
        P("tm"),
        P(None, None, "tp"),
        P("tp", None),
        P(None, None, "tp"),
    )
    return jax.shard_map(
        body, mesh=mesh, in_specs=placed, out_specs=P("tm", None, "tp"), check_vma=False
    )
```

profile of v0, /device:TPU:103, one launch (start us, length us, event | category | flops | bytes accessed | tf_op | source)
XLA Modules:
  0.0 483.2 jit_solution(12489201418532556773)
XLA Ops:
  7.3 2.4 copy.33
  11.3 18.7 %copy.34 = bf16[3072,3,768]{0,2,1:T(8,128)(2,1)} copy(bf16[3072,3,768]{2,0,1:T(8,128)(2,1)} %param.15) | data formatting | bytes 28311552 | tf_op args[3]
  30.7 1.4 dynamic-update-slice
  32.0 8.7 %all-reduce = s32[32]{0:T(128)S(1)} all-reduce(s32[32]{0:T(128)S(1)} %dynamic-update-slice), channel_id=1, replica_groups=mesh['tm'=32,'tp'=4] {'tm'}, use_global_device_ids=true, to_apply=%add | all-reduce | flops 32 | bytes 256
  40.7 40.6 %while.33 = (s32[]{:T(128)}, s32[]{:T(128)}, s32[]{:T(128)}, s32[32]{0:T(128)S(1)}, s32[]{:T(128)}) while((s32[]{:T(128)}, s32[]{:T(128)}, s32[]{:T(128)}, s32[32]{0:T(128)S(1)}, s32[]{:T(128)}) %tuple.62), condition=%wide.region_2.3_spmd, body=%wide.region_1.2_spmd.sunk | while | flops 5 | bytes 107 | solution.py:22
  81.5 2.5 fusion.55
  84.0 20.4 %all-gather.6.cloned.1.call-done = bf16[256,3,3072]{0,2,1:T(8,128)(2,1)} async-done(((bf16[256,3,768]{0,2,1:T(8,128)(2,1)}), bf16[256,3,3072]{0,2,1:T(8,128)(2,1)}) %all-gather.6.cloned.1.call-update) | async-done | bytes 4718608 | tf_op jit(solution)/shard_map/all_gather | solution.py:62
  104.4 3.6 fusion.2
  108.1 10.1 %convolution_convert_fusion.1 = bf16[2,128,2304]{2,1,0:T(8,128)(2,1)} fusion(bf16[3072,2304,1]{0,1,2:T(8,128)(2,1)} %bitcast.116, f32[2,128,3072]{2,1,0:T(8,128)S(1)} %copy-done, f32[2,3072]{1,0:T(2,128)S(1)} %get-tuple-element.162, f32[2,3072]{1,0:T(2,128)S(1)} %get-tuple-element.163, f32[2,128]{1,0:T(2,128)S(1)} %get-tuple-element.167, ...), kind=kOutput, calls=%fused_computation.13 | convolution fusion | flops 3628400640 | bytes 18532352 | tf_op jit(solution)/shard_map/std,de->ste/dot_general | solution.py:84
  118.2 1.7 copy.36
  121.0 4.9 %fusion.8 = bf16[2,128,3072]{2,1,0:T(8,128)(2,1)} fusion(bf16[2,128,768]{1,2,0:T(8,128)(2,1)S(1)} %bitcast.125, bf16[768,3072]{1,0:T(8,128)(2,1)} %param.16), kind=kOutput, calls=%fused_computation.10 | convolution fusion | flops 1208745984 | bytes 6684672 | tf_op jit(solution)/shard_map/sqe,ed->sqd/dot_general | solution.py:99
  126.0 25.2 %reduce-scatter.3.cloned.1.call-done = bf16[2,128,768]{2,1,0:T(8,128)(2,1)} async-done(((bf16[2,128,3072]{2,1,0:T(8,128)(2,1)}), bf16[2,128,768]{2,1,0:T(8,128)(2,1)}) %reduce-scatter.3.cloned.1.call-update) | async-done | bytes 393232 | tf_op jit(solution)/shard_map/reduce_scatter | solution.py:102
  151.2 1.1 fusion.30
  154.0 47.3 %all-gather.10.cloned.1.call-done = bf16[32,128,768]{2,1,0:T(8,128)(2,1)} async-done(((bf16[1,128,768]{2,1,0:T(8,128)(2,1)}), bf16[32,128,768]{2,1,0:T(8,128)(2,1)}) %all-gather.10.cloned.1.call-update) | async-done | bytes 6291472 | tf_op jit(solution)/shard_map/all_gather | solution.py:32
  201.3 31.9 %while.34 = (s32[]{:T(128)}, f32[128,768]{1,0:T(8,128)S(1)}, s32[]{:T(128)}, bf16[32,128,768]{2,1,0:T(8,128)(2,1)}, s32[]{:T(128)}, /*index=5*/s32[]{:T(128)}, s32[]{:T(128)}) while((s32[]{:T(128)}, f32[128,768]{1,0:T(8,128)S(1)}, s32[]{:T(128)}, bf16[32,128,768]{2,1,0:T(8,128)(2,1)}, s32[]{:T(128)}, /*index=5*/s32[]{:T(128)}, ...), condition=%wide.region_11.12_spmd, body=%wide.region_10.11_spmd.sunk | while | flops 196613 | bytes 983155 | solution.py:38
  201.3 1.0 convert_add_fusion.4
  202.4 1.0 convert_add_fusion.4
  203.4 1.0 convert_add_fusion.4
  204.4 1.0 convert_add_fusion.4
  205.5 1.0 convert_add_fusion.4
  206.5 1.0 convert_add_fusion.4
  207.5 1.0 convert_add_fusion.4
  208.5 1.0 convert_add_fusion.4
  209.6 1.0 convert_add_fusion.4
  211.6 1.0 convert_add_fusion.4
  212.7 1.0 convert_add_fusion.4
  213.7 1.0 convert_add_fusion.4
  214.7 1.0 convert_add_fusion.4
  215.7 1.0 convert_add_fusion.4
  216.8 1.0 convert_add_fusion.4
  217.8 1.0 convert_add_fusion.4
  218.8 1.0 convert_add_fusion.4
  219.9 1.0 convert_add_fusion.4
  220.9 1.0 convert_add_fusion.4
  221.9 1.0 convert_add_fusion.4
  223.0 1.0 convert_add_fusion.4
  224.0 1.0 convert_add_fusion.4
  225.0 1.0 convert_add_fusion.4
  226.0 1.0 convert_add_fusion.4
  227.1 1.0 convert_add_fusion.4
  228.1 1.0 convert_add_fusion.4
  229.1 1.0 convert_add_fusion.4
  230.2 1.0 convert_add_fusion.4
  231.2 1.0 convert_add_fusion.4
  232.2 1.0 convert_add_fusion.4
  233.2 73.6 %all-reduce.3.cloned.1.call-done = f32[128,768]{1,0:T(8,128)} async-done(((f32[128,768]{1,0:T(8,128)}), f32[128,768]{1,0:T(8,128)}) %all-reduce.3.cloned.1.call-update) | async-done | bytes 393232 | tf_op jit(solution)/shard_map/psum | solution.py:27
  306.8 1.0 add.136
  309.1 40.2 %all-gather.12.cloned.1.call-done = f32[2,128,3072]{2,1,0:T(8,128)} async-done(((f32[2,128,768]{2,1,0:T(8,128)}), f32[2,128,3072]{2,1,0:T(8,128)}) %all-gather.12.cloned.1.call-update) | async-done | bytes 3145744 | tf_op jit(solution)/shard_map/all_gather | solution.py:74
  349.3 2.6 fusion.54
  352.1 9.1 %convolution_convert_fusion = bf16[2,128,2304]{2,1,0:T(8,128)(2,1)S(1)} fusion(bf16[3072,2304,1]{0,1,2:T(8,128)(2,1)} %bitcast.117, f32[2,128,3072]{2,1,0:T(8,128)S(1)} %copy-done.1, f32[2,128]{1,0:T(2,128)S(1)} %get-tuple-element.165, f32[2,128]{1,0:T(2,128)S(1)} %get-tuple-element.164, f32[2,3072]{1,0:T(2,128)S(1)} %get-tuple-element.162, ...), kind=kOutput, calls=%fused_computation.12 | convolution fusion | flops 3628400640 | bytes 18532352 | tf_op jit(solution)/shard_map/std,de->ste/dot_general | solution.py:84
  363.1 4.9 %fusion.11 = bf16[2,128,3072]{2,1,0:T(8,128)(2,1)} fusion(bf16[2,128,768]{1,2,0:T(8,128)(2,1)S(1)} %bitcast.126, bf16[768,3072]{1,0:T(8,128)(2,1)} %param.16), kind=kOutput, calls=%fused_computation.11 | convolution fusion | flops 1208745984 | bytes 6684672 | tf_op jit(solution)/shard_map/sqe,ed->sqd/dot_general | solution.py:99
  368.1 25.1 %reduce-scatter.5.cloned.1.call-done = bf16[2,128,768]{2,1,0:T(8,128)(2,1)} async-done(((bf16[2,128,3072]{2,1,0:T(8,128)(2,1)}), bf16[2,128,768]{2,1,0:T(8,128)(2,1)}) %reduce-scatter.5.cloned.1.call-update) | async-done | bytes 393232 | tf_op jit(solution)/shard_map/reduce_scatter | solution.py:102
  393.2 1.1 fusion.26
  395.0 48.4 %all-gather.14.cloned.1.call-done = bf16[32,128,768]{2,1,0:T(8,128)(2,1)} async-done(((bf16[1,128,768]{2,1,0:T(8,128)(2,1)}), bf16[32,128,768]{2,1,0:T(8,128)(2,1)}) %all-gather.14.cloned.1.call-update) | async-done | bytes 6291472 | tf_op jit(solution)/shard_map/all_gather | solution.py:32
  443.5 31.9 %while.35 = (s32[]{:T(128)}, f32[128,768]{1,0:T(8,128)S(1)}, s32[]{:T(128)}, bf16[32,128,768]{2,1,0:T(8,128)(2,1)}, s32[]{:T(128)}, /*index=5*/s32[]{:T(128)}, s32[]{:T(128)}) while((s32[]{:T(128)}, f32[128,768]{1,0:T(8,128)S(1)}, s32[]{:T(128)}, bf16[32,128,768]{2,1,0:T(8,128)(2,1)}, s32[]{:T(128)}, /*index=5*/s32[]{:T(128)}, ...), condition=%wide.region_20.21_spmd, body=%wide.region_19.20_spmd.sunk | while | flops 196613 | bytes 983155 | solution.py:38
  443.5 1.0 convert_add_fusion.5
  444.5 1.0 convert_add_fusion.5
  445.5 1.0 convert_add_fusion.5
  447.6 1.0 convert_add_fusion.5
  448.6 1.0 convert_add_fusion.5
  449.7 1.0 convert_add_fusion.5
  450.7 1.0 convert_add_fusion.5
  451.7 1.0 convert_add_fusion.5
  452.7 1.0 convert_add_fusion.5
  (111 shorter events, 52.9 us)
Async XLA Ops:
  6.5 3.3 copy-start.4
  6.5 75.0 %all-gather.8.cloned.1.call-start = ((), (), s32[]{:S(2)}) async-start(), calls=%async_computation.3 | async-start | bytes 3932160 | tf_op jit(solution)/shard_map/all_gather | solution.py:74
  7.3 97.2 %all-gather.6.cloned.1.call-start = ((), (), s32[]{:S(2)}) async-start(), calls=%async_computation.2 | async-start | bytes 5898240 | tf_op jit(solution)/shard_map/all_gather | solution.py:62
  9.7 141.5 %reduce-scatter.3.cloned.1.call-start = ((), (), s32[]{:S(2)}) async-start(), calls=%async_computation.4 | async-start | bytes 1966080 | tf_op jit(solution)/shard_map/reduce_scatter | solution.py:102
  11.3 18.7 %copy-start.5 = (u32[128]{0:T(128)S(1)}, u32[128]{0:T(128)}, u32[]{:S(2)}) copy-start(u32[128]{0:T(128)} %constant.91) | copy-start | bytes 1540
  84.0 24.1 %copy-start = (f32[2,128,3072]{2,1,0:T(8,128)S(1)}, f32[2,128,3072]{2,1,0:T(8,128)}, u32[]{:S(2)}) copy-start(f32[2,128,3072]{2,1,0:T(8,128)} %all-gather.8.cloned.1.call-done) | copy-start | bytes 9437188
  125.9 27.2 %copy-start.2 = (f32[2,128,768]{2,1,0:T(8,128)S(1)}, f32[2,128,768]{2,1,0:T(8,128)}, u32[]{:S(2)}) copy-start(f32[2,128,768]{2,1,0:T(8,128)} %param.12) | copy-start | bytes 2359300
  125.9 75.4 %all-gather.10.cloned.1.call-start = ((), (), s32[]{:S(2)}) async-start(), calls=%async_computation.5 | async-start | bytes 6488064 | tf_op jit(solution)/shard_map/all_gather | solution.py:32
  153.0 153.8 %all-reduce.3.cloned.1.call-start = ((), (), s32[]{:S(2)}) async-start(), calls=%async_computation.6 | async-start | bytes 786432 | tf_op jit(solution)/shard_map/psum | solution.py:27
  153.9 195.4 %all-gather.12.cloned.1.call-start = ((), (), s32[]{:S(2)}) async-start(), calls=%async_computation.7 | async-start | bytes 3932160 | tf_op jit(solution)/shard_map/all_gather | solution.py:74
  308.9 84.3 %reduce-scatter.5.cloned.1.call-start = ((), (), s32[]{:S(2)}) async-start(), calls=%async_computation.8 | async-start | bytes 1966080 | tf_op jit(solution)/shard_map/reduce_scatter | solution.py:102
  349.3 2.8 copy-start.1
  368.1 75.4 %all-gather.14.cloned.1.call-start = ((), (), s32[]{:S(2)}) async-start(), calls=%async_computation.9 | async-start | bytes 6488064 | tf_op jit(solution)/shard_map/all_gather | solution.py:32
  394.3 81.1 %copy-start.3 = (f32[128,768]{1,0:T(8,128)S(1)}, f32[128,768]{1,0:T(8,128)}, u32[]{:S(2)}) copy-start(f32[128,768]{1,0:T(8,128)} %all-reduce.3.cloned.1.call-done) | copy-start | bytes 1179652
Sparse Core Ops, SparseCore 0:
  9.0 40.7 all-gather.7
  51.5 52.8 all-gather.5
  126.0 25.1 reduce-scatter.2
  153.3 47.9 all-gather.9
  204.4 102.4 all-reduce.2
  309.0 40.2 all-gather.11
  368.2 24.9 reduce-scatter.4
  395.4 47.9 all-gather.13
where the time goes:
time: 486 us; the launch traced here: 483 us
  waiting for transfers between devices  281 us (58%)
  other arithmetic  74.2 us (15%)
  local copies, waits for them, and re-layouts  46.7 us (10%)
  matrix products  34.9 us (7%)
  loops' own time  22.8 us (5%)
  between operations  14.4 us (3%)
  blocking collectives  8.69 us (2%)
    all_gather x2, waiting for transfers between devices, prefix_2(): gathered = lax.all_gather(array.astype(jnp.bfloat16), axis)  95.7 us
    psum x1, waiting for transfers between devices, broadcast(): return lax.psum(block, axis)  73.6 us
    add x62, other arithmetic, add_up(): return earlier + later  62.1 us
    reduce_scatter x2, waiting for transfers between devices, body(): lax.psum_scatter(head_out.astype(jnp.bfloat16), 'tp', scatter_dimension=2...  50.3 us
    all_gather x2, waiting for transfers between devices, body(): whole_rows = lax.all_gather(states, 'tp', axis=2, tiled=True)  40.2 us
    unnamed x17, local copies, waits for them, and re-layouts  23.4 us
    another operation x1, loops' own time, prefix(): return lax.fori_loop(0, size, turn, start)  21.1 us
    all_gather x1, waiting for transfers between devices, body(): full_mod = lax.all_gather(mod_weight, 'tp', axis=2, tiled=True)  20.4 us
  transfers between devices with their start and end apart: 8, of which 7 were waited for; matrix products, arithmetic and copies ran while one was open for 16% of the time, Pallas kernels for 0%

commit v1 on v0

--- a/solution.py
+++ b/solution.py
@@ -24,7 +24,7 @@
 
 def broadcast(block, axis, holder):
     block = jnp.where(lax.axis_index(axis) == holder, block, jnp.zeros_like(block))
-    return lax.psum(block, axis)
+    return jnp.sum(lax.all_gather(block, axis), axis=0)
 
 
 def prefix_2(array, axis, join, neutral):

time: 486 us -> 450 us (0.926)
  waiting for transfers between devices: 281 us -> 239 us
    psum x1 -> x0, waiting for transfers between devices: 73.6 us -> none  [broadcast(): return lax.psum(block, axis)]
    all_gather x0 -> x1, waiting for transfers between devices: none -> 32.3 us  [broadcast(): return jnp.sum(lax.all_gather(block, axis), axis=0)]
    reduce_sum x0 -> x1, other arithmetic: none -> 5.28 us  [broadcast(): return jnp.sum(lax.all_gather(block, axis), axis=0)]
    unnamed x17 -> x13, local copies, waits for them, and re-layouts: 23.4 us -> 23.1 us
  transfers between devices with their start and end apart: 8 -> 8, of which waited for: 7 -> 7; matrix products, arithmetic and copies ran while one was open for 16% -> 18% of each run, Pallas kernels for 0% -> 0%
where the time goes in v1:
time: 450 us; the launch traced here: 447 us
  waiting for transfers between devices  239 us (53%)
  other arithmetic  78.4 us (17%)
  local copies, waits for them, and re-layouts  47.4 us (11%)
  matrix products  35.7 us (8%)
  loops' own time  22.5 us (5%)
  between operations  14.4 us (3%)
  blocking collectives  8.69 us (2%)
    all_gather x2, waiting for transfers between devices, prefix_2(): gathered = lax.all_gather(array.astype(jnp.bfloat16), axis)  95.9 us
    add x62, other arithmetic, add_up(): return earlier + later  62.1 us
    reduce_scatter x2, waiting for transfers between devices, body(): lax.psum_scatter(head_out.astype(jnp.bfloat16), 'tp', scatter_dimension=2...  50.3 us
    all_gather x2, waiting for transfers between devices, body(): whole_rows = lax.all_gather(states, 'tp', axis=2, tiled=True)  40.7 us
    all_gather x1, waiting for transfers between devices, broadcast(): return jnp.sum(lax.all_gather(block, axis), axis=0)  32.3 us
    unnamed x13, local copies, waits for them, and re-layouts  23.1 us
    another operation x1, loops' own time, prefix(): return lax.fori_loop(0, size, turn, start)  21.1 us
    dynamic_slice x32, local copies, waits for them, and re-layouts, turn(): new = combine(before, everything[k])  20.4 us
  transfers between devices with their start and end apart: 8, of which 7 were waited for; matrix products, arithmetic and copies ran while one was open for 18% of the time, Pallas kernels for 0%

profile of v1, /device:TPU:103, one launch (start us, length us, event | category | flops | bytes accessed | tf_op | source)
XLA Modules:
  0.0 446.9 jit_solution(8175566197336938386)
XLA Ops:
  7.3 2.4 copy.33
  11.3 18.7 %copy.34 = bf16[3072,3,768]{0,2,1:T(8,128)(2,1)} copy(bf16[3072,3,768]{2,0,1:T(8,128)(2,1)} %param.15) | data formatting | bytes 28311552 | tf_op args[3]
  30.7 1.4 dynamic-update-slice
  32.0 8.7 %all-reduce = s32[32]{0:T(128)S(1)} all-reduce(s32[32]{0:T(128)S(1)} %dynamic-update-slice), channel_id=1, replica_groups=mesh['tm'=32,'tp'=4] {'tm'}, use_global_device_ids=true, to_apply=%add | all-reduce | flops 32 | bytes 256
  40.7 41.4 %while.33 = (s32[]{:T(128)}, s32[]{:T(128)}, s32[]{:T(128)}, s32[32]{0:T(128)S(1)}, s32[]{:T(128)}) while((s32[]{:T(128)}, s32[]{:T(128)}, s32[]{:T(128)}, s32[32]{0:T(128)S(1)}, s32[]{:T(128)}) %tuple.62), condition=%wide.region_2.3_spmd, body=%wide.region_1.2_spmd.sunk | while | flops 5 | bytes 115 | solution.py:22
  82.3 2.5 fusion.55
  84.9 19.4 %all-gather.7.cloned.1.call-done = bf16[256,3,3072]{0,2,1:T(8,128)(2,1)} async-done(((bf16[256,3,768]{0,2,1:T(8,128)(2,1)}), bf16[256,3,3072]{0,2,1:T(8,128)(2,1)}) %all-gather.7.cloned.1.call-update) | async-done | bytes 4718608 | tf_op jit(solution)/shard_map/all_gather | solution.py:62
  104.3 3.6 fusion.2
  108.0 10.1 %convolution_convert_fusion.1 = bf16[2,128,2304]{2,1,0:T(8,128)(2,1)} fusion(bf16[3072,2304,1]{0,1,2:T(8,128)(2,1)} %bitcast.114, f32[2,128,3072]{2,1,0:T(8,128)S(1)} %copy-done, f32[2,3072]{1,0:T(2,128)S(1)} %get-tuple-element.162, f32[2,3072]{1,0:T(2,128)S(1)} %get-tuple-element.163, f32[2,128]{1,0:T(2,128)S(1)} %get-tuple-element.167, ...), kind=kOutput, calls=%fused_computation.13 | convolution fusion | flops 3628400640 | bytes 18532352 | tf_op jit(solution)/shard_map/std,de->ste/dot_general | solution.py:84
  118.0 1.7 copy.36
  120.9 4.9 %fusion.8 = bf16[2,128,3072]{2,1,0:T(8,128)(2,1)} fusion(bf16[2,128,768]{1,2,0:T(8,128)(2,1)S(1)} %bitcast.123, bf16[768,3072]{1,0:T(8,128)(2,1)} %param.16), kind=kOutput, calls=%fused_computation.10 | convolution fusion | flops 1208745984 | bytes 6684672 | tf_op jit(solution)/shard_map/sqe,ed->sqd/dot_general | solution.py:99
  125.9 25.3 %reduce-scatter.3.cloned.1.call-done = bf16[2,128,768]{2,1,0:T(8,128)(2,1)} async-done(((bf16[2,128,3072]{2,1,0:T(8,128)(2,1)}), bf16[2,128,768]{2,1,0:T(8,128)(2,1)}) %reduce-scatter.3.cloned.1.call-update) | async-done | bytes 393232 | tf_op jit(solution)/shard_map/reduce_scatter | solution.py:102
  151.1 1.1 fusion.30
  153.9 47.4 %all-gather.11.cloned.1.call-done = bf16[32,128,768]{2,1,0:T(8,128)(2,1)} async-done(((bf16[1,128,768]{2,1,0:T(8,128)(2,1)}), bf16[32,128,768]{2,1,0:T(8,128)(2,1)}) %all-gather.11.cloned.1.call-update) | async-done | bytes 6291472 | tf_op jit(solution)/shard_map/all_gather | solution.py:32
  201.3 31.8 %while.34 = (s32[]{:T(128)}, f32[128,768]{1,0:T(8,128)S(1)}, s32[]{:T(128)}, bf16[32,128,768]{2,1,0:T(8,128)(2,1)}, s32[]{:T(128)}, /*index=5*/s32[]{:T(128)}, s32[]{:T(128)}) while((s32[]{:T(128)}, f32[128,768]{1,0:T(8,128)S(1)}, s32[]{:T(128)}, bf16[32,128,768]{2,1,0:T(8,128)(2,1)}, s32[]{:T(128)}, /*index=5*/s32[]{:T(128)}, ...), condition=%wide.region_11.12_spmd, body=%wide.region_10.11_spmd.sunk | while | flops 196613 | bytes 983163 | solution.py:38
  201.3 1.0 convert_add_fusion.4
  202.3 1.0 convert_add_fusion.4
  203.4 1.0 convert_add_fusion.4
  204.4 1.0 convert_add_fusion.4
  205.4 1.0 convert_add_fusion.4
  206.4 1.0 convert_add_fusion.4
  207.5 1.0 convert_add_fusion.4
  208.5 1.0 convert_add_fusion.4
  209.5 1.0 convert_add_fusion.4
  210.5 1.0 convert_add_fusion.4
  211.6 1.0 convert_add_fusion.4
  212.6 1.0 convert_add_fusion.4
  213.6 1.0 convert_add_fusion.4
  214.6 1.0 convert_add_fusion.4
  215.7 1.0 convert_add_fusion.4
  216.7 1.0 convert_add_fusion.4
  217.7 1.0 convert_add_fusion.4
  218.7 1.0 convert_add_fusion.4
  219.8 1.0 convert_add_fusion.4
  220.8 1.0 convert_add_fusion.4
  221.8 1.0 convert_add_fusion.4
  222.9 1.0 convert_add_fusion.4
  223.9 1.0 convert_add_fusion.4
  224.9 1.0 convert_add_fusion.4
  225.9 1.0 convert_add_fusion.4
  227.0 1.0 convert_add_fusion.4
  228.0 1.0 convert_add_fusion.4
  229.0 1.0 convert_add_fusion.4
  230.0 1.0 convert_add_fusion.4
  231.1 1.0 convert_add_fusion.4
  232.1 1.0 convert_add_fusion.4
  233.1 32.3 %all-gather.13.cloned.1.call-done = f32[32,128,768]{2,1,0:T(8,128)} async-done(((f32[1,128,768]{2,1,0:T(8,128)}), f32[32,128,768]{2,1,0:T(8,128)}) %all-gather.13.cloned.1.call-update) | async-done | bytes 12582928 | tf_op jit(solution)/shard_map/all_gather | solution.py:27
  265.4 5.3 %reduce_sum.76 = f32[128,768]{1,0:T(8,128)S(1)} reduce(f32[32,128,768]{2,1,0:T(8,128)} %all-gather.13.cloned.1.call-done, f32[]{:T(128)} %constant.73.clone.1), dimensions={0}, to_apply=%region_12.13 | reduce | flops 3047424 | bytes 12976132 | tf_op jit(solution)/shard_map/reduce_sum | solution.py:27
  272.0 40.7 %all-gather.15.cloned.1.call-done = f32[2,128,3072]{2,1,0:T(8,128)} async-done(((f32[2,128,768]{2,1,0:T(8,128)}), f32[2,128,3072]{2,1,0:T(8,128)}) %all-gather.15.cloned.1.call-update) | async-done | bytes 3145744 | tf_op jit(solution)/shard_map/all_gather | solution.py:74
  312.6 2.4 fusion.54
  315.1 10.0 %convolution_convert_fusion = bf16[2,128,2304]{2,1,0:T(8,128)(2,1)S(1)} fusion(bf16[3072,2304,1]{0,1,2:T(8,128)(2,1)} %bitcast.115, f32[2,128,3072]{2,1,0:T(8,128)} %all-gather.15.cloned.1.call-done, f32[2,128]{1,0:T(2,128)S(1)} %get-tuple-element.165, f32[2,128]{1,0:T(2,128)S(1)} %get-tuple-element.164, f32[2,3072]{1,0:T(2,128)S(1)} %get-tuple-element.162, ...), kind=kOutput, calls=%fused_computation.12 | convolution fusion | flops 3628400640 | bytes 18532352 | tf_op jit(solution)/shard_map/std,de->ste/dot_general | solution.py:84
  327.0 4.9 %fusion.11 = bf16[2,128,3072]{2,1,0:T(8,128)(2,1)} fusion(bf16[2,128,768]{1,2,0:T(8,128)(2,1)S(1)} %bitcast.124, bf16[768,3072]{1,0:T(8,128)(2,1)} %param.16), kind=kOutput, calls=%fused_computation.11 | convolution fusion | flops 1208745984 | bytes 6684672 | tf_op jit(solution)/shard_map/sqe,ed->sqd/dot_general | solution.py:99
  331.9 25.0 %reduce-scatter.5.cloned.1.call-done = bf16[2,128,768]{2,1,0:T(8,128)(2,1)} async-done(((bf16[2,128,3072]{2,1,0:T(8,128)(2,1)}), bf16[2,128,768]{2,1,0:T(8,128)(2,1)}) %reduce-scatter.5.cloned.1.call-update) | async-done | bytes 393232 | tf_op jit(solution)/shard_map/reduce_scatter | solution.py:102
  357.0 1.1 fusion.26
  358.8 48.5 %all-gather.17.cloned.1.call-done = bf16[32,128,768]{2,1,0:T(8,128)(2,1)} async-done(((bf16[1,128,768]{2,1,0:T(8,128)(2,1)}), bf16[32,128,768]{2,1,0:T(8,128)(2,1)}) %all-gather.17.cloned.1.call-update) | async-done | bytes 6291472 | tf_op jit(solution)/shard_map/all_gather | solution.py:32
  407.3 31.7 %while.35 = (s32[]{:T(128)}, f32[128,768]{1,0:T(8,128)S(1)}, s32[]{:T(128)}, bf16[32,128,768]{2,1,0:T(8,128)(2,1)}, s32[]{:T(128)}, /*index=5*/s32[]{:T(128)}, s32[]{:T(128)}) while((s32[]{:T(128)}, f32[128,768]{1,0:T(8,128)S(1)}, s32[]{:T(128)}, bf16[32,128,768]{2,1,0:T(8,128)(2,1)}, s32[]{:T(128)}, /*index=5*/s32[]{:T(128)}, ...), condition=%wide.region_20.21_spmd, body=%wide.region_19.20_spmd.sunk | while | flops 196613 | bytes 983163 | solution.py:38
  407.4 1.0 convert_add_fusion.5
  408.4 1.0 convert_add_fusion.5
  409.4 1.0 convert_add_fusion.5
  410.4 1.0 convert_add_fusion.5
  411.5 1.0 convert_add_fusion.5
  412.5 1.0 convert_add_fusion.5
  413.5 1.0 convert_add_fusion.5
  414.5 1.0 convert_add_fusion.5
  (108 shorter events, 53.6 us)
Async XLA Ops:
  6.5 3.9 copy-start.2
  6.5 75.8 %all-gather.9.cloned.1.call-start = ((), (), s32[]{:S(2)}) async-start(), calls=%async_computation.3 | async-start | bytes 3932160 | tf_op jit(solution)/shard_map/all_gather | solution.py:74
  7.3 97.0 %all-gather.7.cloned.1.call-start = ((), (), s32[]{:S(2)}) async-start(), calls=%async_computation.2 | async-start | bytes 5898240 | tf_op jit(solution)/shard_map/all_gather | solution.py:62
  9.7 141.4 %reduce-scatter.3.cloned.1.call-start = ((), (), s32[]{:S(2)}) async-start(), calls=%async_computation.4 | async-start | bytes 1966080 | tf_op jit(solution)/shard_map/reduce_scatter | solution.py:102
  11.3 18.7 %copy-start.3 = (u32[128]{0:T(128)S(1)}, u32[128]{0:T(128)}, u32[]{:S(2)}) copy-start(u32[128]{0:T(128)} %constant.91) | copy-start | bytes 1540
  84.8 23.1 %copy-start = (f32[2,128,3072]{2,1,0:T(8,128)S(1)}, f32[2,128,3072]{2,1,0:T(8,128)}, u32[]{:S(2)}) copy-start(f32[2,128,3072]{2,1,0:T(8,128)} %all-gather.9.cloned.1.call-done) | copy-start | bytes 9437188
  125.8 27.3 %copy-start.1 = (f32[2,128,768]{2,1,0:T(8,128)S(1)}, f32[2,128,768]{2,1,0:T(8,128)}, u32[]{:S(2)}) copy-start(f32[2,128,768]{2,1,0:T(8,128)} %param.12) | copy-start | bytes 2359300
  125.8 75.5 %all-gather.11.cloned.1.call-start = ((), (), s32[]{:S(2)}) async-start(), calls=%async_computation.5 | async-start | bytes 6488064 | tf_op jit(solution)/shard_map/all_gather | solution.py:32
  153.0 112.4 %all-gather.13.cloned.1.call-start = ((), (), s32[]{:S(2)}) async-start(), calls=%async_computation.6 | async-start | bytes 12976128 | tf_op jit(solution)/shard_map/all_gather | solution.py:27
  153.8 158.8 %all-gather.15.cloned.1.call-start = ((), (), s32[]{:S(2)}) async-start(), calls=%async_computation.7 | async-start | bytes 3932160 | tf_op jit(solution)/shard_map/all_gather | solution.py:74
  271.8 85.2 %reduce-scatter.5.cloned.1.call-start = ((), (), s32[]{:S(2)}) async-start(), calls=%async_computation.8 | async-start | bytes 1966080 | tf_op jit(solution)/shard_map/reduce_scatter | solution.py:102
  331.9 75.4 %all-gather.17.cloned.1.call-start = ((), (), s32[]{:S(2)}) async-start(), calls=%async_computation.9 | async-start | bytes 6488064 | tf_op jit(solution)/shard_map/all_gather | solution.py:32
Sparse Core Ops, SparseCore 0:
  9.0 40.7 all-gather.8
  51.5 52.7 all-gather.6
  125.9 25.1 reduce-scatter.2
  153.2 47.9 all-gather.10
  203.4 61.9 all-gather.12
  271.9 40.7 all-gather.14
  332.0 24.8 reduce-scatter.4
  359.2 48.0 all-gather.16
